TPU v7x, 256 devices: a whole 4x4x8 slice. The times are simulated.
256 devices in a mesh: fn: 8 (over z_hi, core), pt: 32 (over x, y, z_lo).
Axes of the slice: x: 4, y: 4, z: 8 (z_hi: 4, z_lo: 2; z = z_hi * 2 + z_lo), core: 2. Of those that a mesh axis runs over, the one named last changes fastest.
Arguments:
- functions: bfloat16 [16384, 4096], P(('fn', 'pt')), may hold values from -6 to 6
- branch_in: bfloat16 [4096, 256], replicated, may hold values from -0.09375 to 0.09375
- branch_out: bfloat16 [256, 128], replicated, may hold values from -0.375 to 0.375
- branch_tangent: bfloat16 [256, 128], replicated, may hold values from -0.375 to 0.375
- points: float32 [2, 32768], P(None, ('pt', 'fn')), may hold values from 0 to 1
- trunk_in: float32 [2, 256], replicated, may hold values from -4 to 4
- trunk_bias: float32 [256], replicated, may hold values from -1 to 1
- trunk_out: bfloat16 [256, 128], replicated, may hold values from -0.375 to 0.375
- trunk_tangent: bfloat16 [256, 128], replicated, may hold values from -0.375 to 0.375
- slopes: bfloat16 [2, 16384, 32768], P(None, 'fn', 'pt'), may hold values from -4 to 4
Outputs:
- row_grad: float32 [16384, 128], P(('fn', 'pt'))
- branch_grad: float32 [256, 128], replicated
- trunk_grad: float32 [256, 128], replicated
All inputs are finite; a program needn't handle non-finite values.
Results may differ from a plain program's by a relative error of at most 0.0041.
Values may be sent and summed in bfloat16 or wider, within the bound.
No kernel may reach another device: no remote copies, remote signals or barrier semaphores. Data moves between devices by JAX's collectives and lax.ppermute only.
A program may use at most 192 MiB of HBM per device.

v0:
```python
import jax
import jax.numpy as jnp
from jax import lax
from jax.sharding import PartitionSpec as P


def jet_features(points, trunk_in, trunk_bias):
    preact = (
        points[0][:, None] * trunk_in[0][None, :]
        + points[1][:, None] * trunk_in[1][None, :]
        + trunk_bias[None, :]
    )
    tanh_value = jnp.tanh(preact)
    first_deriv = 1.0 - tanh_value * tanh_value
    second_deriv = -2.0 * tanh_value * first_deriv
    square_sum = trunk_in[0] * trunk_in[0] + trunk_in[1] * trunk_in[1]
    return jnp.stack(
        [
            second_deriv * square_sum[None, :],
            first_deriv * trunk_in[0][None, :],
            first_deriv * trunk_in[1][None, :],
        ]
    ).astype(jnp.bfloat16)


def project(source, matrix):
    return jnp.einsum("cjk,kp->cjp", source, matrix, preferred_element_type=jnp.float32).astype(
        jnp.bfloat16
    )


def local(
    functions,
    branch_in,
    branch_out,
    branch_tangent,
    points,
    trunk_in,
    trunk_bias,
    trunk_out,
    trunk_tangent,
    slopes,
):
    highest = lax.Precision.HIGHEST
    total_rows = functions.shape[0] * lax.axis_size("fn") * lax.axis_size("pt")
    total_points = points.shape[1] * lax.axis_size("fn") * lax.axis_size("pt")
    hidden = jnp.tanh(jnp.dot(functions, branch_in, preferred_element_type=jnp.float32)).astype(
        jnp.bfloat16
    )
    latent = jnp.dot(hidden, branch_out, preferred_element_type=jnp.float32).astype(jnp.bfloat16)
    latent_tan = jnp.dot(hidden, branch_tangent, preferred_element_type=jnp.float32).astype(
        jnp.bfloat16
    )
    stacked = lax.all_gather(jnp.stack([latent, latent_tan]), "pt", axis=1, tiled=True)
    features = jet_features(points, trunk_in, trunk_bias)
    local_pair = jnp.stack([project(features, trunk_out), project(features, trunk_tangent)])
    gathered = lax.all_gather(local_pair, "fn", axis=2, tiled=True)
    trunk_val = gathered[0]
    trunk_tan = gathered[1]
    row_latent = stacked[0]
    row_factors = jnp.concatenate([stacked[0], stacked[1]], axis=1)
    point_factors = jnp.concatenate([trunk_tan, trunk_val], axis=2)
    response = jnp.einsum(
        "ik,cjk->cij", row_factors, point_factors, preferred_element_type=jnp.float32
    )
    slope_pair = slopes.astype(jnp.float32)
    tangent = response[0] + slope_pair[0] * response[1] + slope_pair[1] * response[2]
    scaled = tangent * (1.0 / total_points)
    weights = jnp.stack([scaled, slope_pair[0] * scaled, slope_pair[1] * scaled]).astype(
        jnp.bfloat16
    )
    weight_block = weights
    row_grad = lax.psum_scatter(
        jnp.einsum("cij,cjp->ip", weight_block, trunk_val, preferred_element_type=jnp.float32),
        "pt",
        scatter_dimension=0,
        tiled=True,
    )
    weight_block = weights
    summed = jnp.einsum("cij,ip->jcp", weight_block, row_latent, preferred_element_type=jnp.float32)
    point_grad = lax.psum_scatter(
        summed * (1.0 / total_rows), "fn", scatter_dimension=0, tiled=True
    )
    trunk_grad = jnp.einsum(
        "cjk,jcp->kp", features.astype(jnp.float32), point_grad, precision=highest
    )
    branch_grad = jnp.dot(hidden.astype(jnp.float32).T, row_grad, precision=highest) * (
        1.0 / total_rows
    )
    branch_grad, trunk_grad = lax.psum((branch_grad, trunk_grad), ("fn", "pt"))
    return (row_grad, branch_grad, trunk_grad)


def solution(mesh):
    in_specs = (
        P(("fn", "pt"), None),
        P(),
        P(),
        P(),
        P(None, ("pt", "fn")),
        P(),
        P(),
        P(),
        P(),
        P(None, "fn", "pt"),
    )
    out_specs = (P(("fn", "pt"), None), P(), P())
    return jax.shard_map(local, mesh=mesh, in_specs=in_specs, out_specs=out_specs, check_vma=False)
```

profile of v0, /device:TPU:2, one launch (start us, length us, event | category | flops | bytes accessed | tf_op | source)
XLA Modules:
  0.0 728.4 jit_solution(10988406394103816467)
XLA Ops:
  7.2 0.0 copy-start
  7.2 0.0 all-gather.5.cloned.1.call-start
  7.2 1.5 copy-done
  8.8 1.5 fusion.11
  10.3 1.0 fusion.13
  11.2 1.0 fusion.12
  12.2 0.6 pad_maximum_fusion.9
  12.9 0.0 all-gather.5.cloned.1.call-update
  12.9 0.0 all-gather.3.cloned.1.call-start
  12.9 0.8 slice_bitcast_fusion.5
  13.7 0.8 multiply_add_fusion
  14.5 0.8 multiply_convert_fusion.4
  15.3 1.0 fusion.10
  16.3 1.0 fusion.9
  17.4 0.7 pad_maximum_fusion.8
  18.1 0.0 all-gather.3.cloned.1.call-update
  18.1 0.0 reduce-scatter.3.cloned.1.call-start
  18.1 11.7 %copy.13 = bf16[2,2048,1024]{1,2,0:T(8,128)(2,1)} copy(bf16[2,2048,1024]{2,1,0:T(8,128)(2,1)} %param.19) | data formatting | bytes 16777216 | tf_op args[9]
  29.9 11.2 %convert_element_type.27 = f32[2,2048,1024]{1,2,0:T(8,128)} convert(bf16[2,2048,1024]{1,2,0:T(8,128)(2,1)} %copy.13) | non-fusion elementwise | flops 4194304 | bytes 25165824 | tf_op jit(solution)/shard_map/convert_element_type | solution.py:66
  41.1 121.1 %all-gather.5.cloned.1.call-done = bf16[2,2048,128]{2,1,0:T(8,128)(2,1)} async-done(((bf16[2,64,128]{2,1,0:T(8,128)(2,1)}), bf16[2,2048,128]{2,1,0:T(8,128)(2,1)}) %all-gather.5.cloned.1.call-update) | async-done | bytes 1048592 | tf_op jit(solution)/shard_map/all_gather | solution.py:54
  162.2 1.3 slice_bitcast_fusion.3
  163.5 41.8 %all-gather.3.cloned.1.call-done = bf16[2,3,1024,128]{3,2,1,0:T(8,128)(2,1)} async-done(((bf16[2,3,128,128]{3,2,1,0:T(8,128)(2,1)}), bf16[2,3,1024,128]{3,2,1,0:T(8,128)(2,1)}) %all-gather.3.cloned.1.call-update) | async-done | bytes 1572880 | tf_op jit(solution)/shard_map/all_gather | solution.py:57
  205.3 1.5 slice_bitcast_fusion.1
  206.8 10.2 %convolution_bitcast_fusion = f32[3,2048,1024]{1,2,0:T(8,128)} fusion(bf16[3,1024,128]{2,1,0:T(8,128)(2,1)S(1)} %get-tuple-element.10, bf16[3,1024,128]{2,1,0:T(8,128)(2,1)S(1)} %get-tuple-element.9, bf16[2048,128]{1,0:T(8,128)(2,1)S(1)} %get-tuple-element.12, bf16[2048,128]{1,0:T(8,128)(2,1)S(1)} %get-tuple-element.11), kind=kOutput, calls=%fused_computation.1 | convolution fusion | flops 3226468352 | bytes 27787264 | tf_op jit(solution)/shard_map/ik,cjk->cij/dot_general | solution.py:63
  217.0 20.8 %fusion.23 = (bf16[1,2048,1024]{1,2,0:T(8,128)(2,1)}, f32[1,2048,1024]{1,2,0:T(8,128)}) fusion(f32[3,2048,1024]{1,2,0:T(8,128)} %convolution_bitcast_fusion, f32[2,2048,1024]{1,2,0:T(8,128)} %convert_element_type.27), kind=kLoop, calls=%fused_computation.53 | loop fusion | flops 12582912 | bytes 54525952 | tf_op jit(solution)/shard_map/convert
  237.9 10.3 %multiply_convert_fusion.1 = (bf16[1,2048,1024]{1,2,0:T(8,128)(2,1)S(1)}, bf16[1,2048,1024]{1,2,0:T(8,128)(2,1)S(1)}) fusion(f32[1,2048,1024]{1,2,0:T(8,128)} %get-tuple-element.6, f32[2,2048,1024]{1,2,0:T(8,128)} %convert_element_type.27), kind=kLoop, calls=%fused_computation.8 | loop fusion | flops 8388608 | bytes 33554432 | tf_op jit(solution)/shard_map/convert.1
  248.2 0.0 copy-start.3
  248.2 0.0 copy-start.4
  248.2 2.0 copy-done.3
  250.2 1.3 copy-done.4
  251.4 0.0 copy-done.2
  251.4 0.0 copy-done.5
  251.4 4.9 fusion.5
  256.3 0.0 reduce-scatter.3.cloned.1.call-update
  256.3 0.0 reduce-scatter.5.cloned.1.call-start
  256.4 0.0 copy-done.6
  256.4 0.0 copy-start.1
  256.4 7.5 %multiply_bitcast_fusion = f32[1024,3,128]{2,0,1:T(8,128)} fusion(bf16[1,2048,1024]{1,2,0:T(8,128)(2,1)} %copy-done.4, bf16[1,2048,1024]{1,2,0:T(8,128)(2,1)} %copy-done.3, bf16[1,2048,1024]{1,2,0:T(8,128)(2,1)} %get-tuple-element.5, bf16[2,2048,128]{2,1,0:T(8,128)(2,1)S(1)} %copy-done.6), kind=kOutput, calls=%fused_computation.15 | convolution fusion | flops 1648754688 | bytes 14680064 | tf_op jit(solution)/shard_map/cij,ip->jcp/dot_general | solution.py:80
  263.9 0.0 reduce-scatter.5.cloned.1.call-update
  264.0 0.0 all-reduce.3.cloned.1.call-start
  264.0 141.1 %reduce-scatter.3.cloned.1.call-done = f32[64,128]{1,0:T(8,128)} async-done(((f32[2048,128]{1,0:T(8,128)}), f32[64,128]{1,0:T(8,128)}) %reduce-scatter.3.cloned.1.call-update) | async-done | bytes 32784 | tf_op jit(solution)/shard_map/reduce_scatter | solution.py:73
  405.1 1.7 convolution_multiply_fusion
  406.8 52.3 %reduce-scatter.5.cloned.1.call-done = f32[128,3,128]{2,0,1:T(8,128)} async-done(((f32[1024,3,128]{2,0,1:T(8,128)}), f32[128,3,128]{2,0,1:T(8,128)}) %reduce-scatter.5.cloned.1.call-update) | async-done | bytes 196624 | tf_op jit(solution)/shard_map/reduce_scatter | solution.py:81
  459.1 2.0 convolution_bitcast_fusion.1
  461.0 0.0 all-reduce.3.cloned.1.call-update
  461.1 257.6 %all-reduce.3.cloned.1.call-done = (f32[256,128]{1,0:T(8,128)}, f32[256,128]{1,0:T(8,128)}) async-done(((f32[256,128]{1,0:T(8,128)}, f32[256,128]{1,0:T(8,128)}), (f32[256,128]{1,0:T(8,128)}, f32[256,128]{1,0:T(8,128)})) %all-reduce.3.cloned.1.call-update) | async-done | bytes 262160 | tf_op jit(solution)/shard_map/psum | solution.py:90
  718.7 1.6 copy.20
  720.3 1.6 copy.21
  (4 shorter events, 0.0 us)
Async XLA Ops:
  7.2 1.6 copy-start
  7.2 155.0 %all-gather.5.cloned.1.call-start = ((), (), s32[]{:S(2)}) async-start(), calls=%async_computation.3 | async-start | bytes 1081344 | tf_op jit(solution)/shard_map/all_gather | solution.py:54
  12.9 192.4 %all-gather.3.cloned.1.call-start = ((), (), s32[]{:S(2)}) async-start(), calls=%async_computation.2 | async-start | bytes 1769472 | tf_op jit(solution)/shard_map/all_gather | solution.py:57
  18.1 387.0 %reduce-scatter.3.cloned.1.call-start = ((), (), s32[]{:S(2)}) async-start(), calls=%async_computation.4 | async-start | bytes 1081344 | tf_op jit(solution)/shard_map/reduce_scatter | solution.py:73
  237.9 13.6 %copy-start.2 = (bf16[1,2048,1024]{1,2,0:T(8,128)(2,1)S(1)}, bf16[1,2048,1024]{1,2,0:T(8,128)(2,1)}, u32[]{:S(2)}) copy-start(bf16[1,2048,1024]{1,2,0:T(8,128)(2,1)} %get-tuple-element.5) | copy-start | bytes 12582916
  237.9 13.6 %copy-start.5 = (bf16[2,3,1024,128]{3,2,1,0:T(8,128)(2,1)S(1)}, bf16[2,3,1024,128]{3,2,1,0:T(8,128)(2,1)}, u32[]{:S(2)}) copy-start(bf16[2,3,1024,128]{3,2,1,0:T(8,128)(2,1)} %all-gather.3.cloned.1.call-done) | copy-start | bytes 4718596
  248.2 2.0 copy-start.3
  248.2 3.3 copy-start.4
  251.4 5.0 copy-start.6
  256.3 202.7 %reduce-scatter.5.cloned.1.call-start = ((), (), s32[]{:S(2)}) async-start(), calls=%async_computation.5 | async-start | bytes 1769472 | tf_op jit(solution)/shard_map/reduce_scatter | solution.py:81
  256.4 465.4 %copy-start.1 = (bf16[4096,256]{1,0:T(8,128)(2,1)S(1)}, bf16[4096,256]{1,0:T(8,128)(2,1)}, u32[]{:S(2)}) copy-start(bf16[4096,256]{1,0:T(8,128)(2,1)} %param.11) | copy-start | bytes 6291460
  264.0 454.7 %all-reduce.3.cloned.1.call-start = ((), (), s32[]{:S(2)}) async-start(), calls=%async_computation.6 | async-start | bytes 524288 | tf_op jit(solution)/shard_map/psum | solution.py:90
Sparse Core Ops, SparseCore 0:
  13.0 149.1 all-gather.4
  164.0 41.2 all-gather.2
  256.5 148.5 reduce-scatter.2
  407.5 51.5 reduce-scatter.4
  465.1 253.5 all-reduce.2
where the time goes:
time: 729 us; the launch traced here: 728 us
  waiting for transfers between devices  614 us (84%)
  other arithmetic  45.3 us (6%)
  matrix products  31.8 us (4%)
  local copies, waits for them, and re-layouts  23.2 us (3%)
  between operations  13.9 us (2%)
    psum x1, waiting for transfers between devices, local(): branch_grad, trunk_grad = lax.psum((branch_grad, trunk_grad), ('fn', 'pt'))  258 us
    reduce_scatter x1, waiting for transfers between devices, local(): lax.psum_scatter(jnp.einsum('cij,cjp->ip', weight_block, trunk_val, prefe...  141 us
    all_gather x1, waiting for transfers between devices, local(): lax.all_gather(jnp.stack([latent, latent_tan]), 'pt', axis=1, tiled=True)  121 us
    reduce_scatter x1, waiting for transfers between devices, local(): lax.psum_scatter(summed * (1.0 / total_rows), 'fn', scatter_dimension=0,...  52.3 us
    all_gather x1, waiting for transfers between devices, local(): gathered = lax.all_gather(local_pair, 'fn', axis=2, tiled=True)  41.8 us
    another operation x3, other arithmetic  31.9 us
    unnamed x17, local copies, waits for them, and re-layouts  19.7 us
  transfers between devices with their start and end apart: 5, of which 5 were waited for; matrix products, arithmetic and copies ran while one was open for 5% of the time, Pallas kernels for 0%

commit v1 on v0

--- a/solution.py
+++ b/solution.py
@@ -87,7 +87,7 @@
     branch_grad = jnp.dot(hidden.astype(jnp.float32).T, row_grad, precision=highest) * (
         1.0 / total_rows
     )
-    branch_grad, trunk_grad = lax.psum((branch_grad, trunk_grad), ("fn", "pt"))
+    branch_grad, trunk_grad = lax.psum(lax.psum((branch_grad, trunk_grad), "pt"), "fn")
     return (row_grad, branch_grad, trunk_grad)
 
 

time: 729 us -> 861 us (1.18)
  waiting for transfers between devices: 614 us -> 745 us
    psum x1 -> x2, waiting for transfers between devices: 258 us -> 389 us  [the longest x1 306 us: local(): lax.psum((branch_grad, trunk_grad), 'pt')]
  transfers between devices with their start and end apart: 5 -> 6, of which waited for: 5 -> 6; matrix products, arithmetic and copies ran while one was open for 5% -> 4% of each run, Pallas kernels for 0% -> 0%
where the time goes in v1:
time: 861 us; the launch traced here: 860 us
  waiting for transfers between devices  745 us (87%)
  other arithmetic  45.3 us (5%)
  matrix products  31.8 us (4%)
  local copies, waits for them, and re-layouts  23.2 us (3%)
  between operations  14.2 us (2%)
    psum x1, waiting for transfers between devices, local(): lax.psum((branch_grad, trunk_grad), 'pt')  306 us
    reduce_scatter x1, waiting for transfers between devices, local(): lax.psum_scatter(jnp.einsum('cij,cjp->ip', weight_block, trunk_val, prefe...  141 us
    all_gather x1, waiting for transfers between devices, local(): lax.all_gather(jnp.stack([latent, latent_tan]), 'pt', axis=1, tiled=True)  121 us
    psum x1, waiting for transfers between devices, local(): lax.psum(lax.psum((branch_grad, trunk_grad), 'pt'), 'fn')  83.4 us
    reduce_scatter x1, waiting for transfers between devices, local(): lax.psum_scatter(summed * (1.0 / total_rows), 'fn', scatter_dimension=0,...  52.2 us
    all_gather x1, waiting for transfers between devices, local(): gathered = lax.all_gather(local_pair, 'fn', axis=2, tiled=True)  41.8 us
    another operation x3, other arithmetic  31.9 us
    unnamed x17, local copies, waits for them, and re-layouts  19.7 us
  transfers between devices with their start and end apart: 6, of which 6 were waited for; matrix products, arithmetic and copies ran while one was open for 4% of the time, Pallas kernels for 0%

profile of v1, /device:TPU:2, one launch (start us, length us, event | category | flops | bytes accessed | tf_op | source)
XLA Modules:
  0.0 860.2 jit_solution(10878410692282850105)
XLA Ops:
  7.2 0.0 copy-start
  7.2 0.0 all-gather.5.cloned.1.call-start
  7.2 1.5 copy-done
  8.8 1.5 fusion.11
  10.3 1.0 fusion.13
  11.2 1.0 fusion.12
  12.2 0.6 pad_maximum_fusion.9
  12.9 0.0 all-gather.5.cloned.1.call-update
  12.9 0.0 all-gather.3.cloned.1.call-start
  12.9 0.8 slice_bitcast_fusion.5
  13.7 0.8 multiply_add_fusion
  14.5 0.8 multiply_convert_fusion.4
  15.3 1.0 fusion.10
  16.3 1.0 fusion.9
  17.4 0.7 pad_maximum_fusion.8
  18.1 0.0 all-gather.3.cloned.1.call-update
  18.1 0.0 reduce-scatter.3.cloned.1.call-start
  18.2 11.8 %copy.13 = bf16[2,2048,1024]{1,2,0:T(8,128)(2,1)} copy(bf16[2,2048,1024]{2,1,0:T(8,128)(2,1)} %param.19) | data formatting | bytes 16777216 | tf_op args[9]
  29.9 11.3 %convert_element_type.27 = f32[2,2048,1024]{1,2,0:T(8,128)} convert(bf16[2,2048,1024]{1,2,0:T(8,128)(2,1)} %copy.13) | non-fusion elementwise | flops 4194304 | bytes 25165824 | tf_op jit(solution)/shard_map/convert_element_type | solution.py:66
  41.2 121.0 %all-gather.5.cloned.1.call-done = bf16[2,2048,128]{2,1,0:T(8,128)(2,1)} async-done(((bf16[2,64,128]{2,1,0:T(8,128)(2,1)}), bf16[2,2048,128]{2,1,0:T(8,128)(2,1)}) %all-gather.5.cloned.1.call-update) | async-done | bytes 1048592 | tf_op jit(solution)/shard_map/all_gather | solution.py:54
  162.2 1.3 slice_bitcast_fusion.3
  163.5 41.8 %all-gather.3.cloned.1.call-done = bf16[2,3,1024,128]{3,2,1,0:T(8,128)(2,1)} async-done(((bf16[2,3,128,128]{3,2,1,0:T(8,128)(2,1)}), bf16[2,3,1024,128]{3,2,1,0:T(8,128)(2,1)}) %all-gather.3.cloned.1.call-update) | async-done | bytes 1572880 | tf_op jit(solution)/shard_map/all_gather | solution.py:57
  205.3 1.5 slice_bitcast_fusion.1
  206.8 10.2 %convolution_bitcast_fusion = f32[3,2048,1024]{1,2,0:T(8,128)} fusion(bf16[3,1024,128]{2,1,0:T(8,128)(2,1)S(1)} %get-tuple-element.12, bf16[3,1024,128]{2,1,0:T(8,128)(2,1)S(1)} %get-tuple-element.11, bf16[2048,128]{1,0:T(8,128)(2,1)S(1)} %get-tuple-element.14, bf16[2048,128]{1,0:T(8,128)(2,1)S(1)} %get-tuple-element.13), kind=kOutput, calls=%fused_computation.1 | convolution fusion | flops 3226468352 | bytes 27787264 | tf_op jit(solution)/shard_map/ik,cjk->cij/dot_general | solution.py:63
  217.0 20.8 %fusion.23 = (bf16[1,2048,1024]{1,2,0:T(8,128)(2,1)}, f32[1,2048,1024]{1,2,0:T(8,128)}) fusion(f32[3,2048,1024]{1,2,0:T(8,128)} %convolution_bitcast_fusion, f32[2,2048,1024]{1,2,0:T(8,128)} %convert_element_type.27), kind=kLoop, calls=%fused_computation.53 | loop fusion | flops 12582912 | bytes 54525952 | tf_op jit(solution)/shard_map/convert
  237.8 10.3 %multiply_convert_fusion.1 = (bf16[1,2048,1024]{1,2,0:T(8,128)(2,1)S(1)}, bf16[1,2048,1024]{1,2,0:T(8,128)(2,1)S(1)}) fusion(f32[1,2048,1024]{1,2,0:T(8,128)} %get-tuple-element.8, f32[2,2048,1024]{1,2,0:T(8,128)} %convert_element_type.27), kind=kLoop, calls=%fused_computation.8 | loop fusion | flops 8388608 | bytes 33554432 | tf_op jit(solution)/shard_map/convert.1
  248.1 0.0 copy-start.3
  248.1 2.0 copy-done.3
  250.1 1.3 copy-done.4
  251.4 0.0 copy-done.5
  251.4 4.9 fusion.5
  256.2 0.0 reduce-scatter.3.cloned.1.call-update
  256.3 0.0 reduce-scatter.5.cloned.1.call-start
  256.3 0.0 copy-start.1
  256.3 7.5 multiply_bitcast_fusion
  263.9 0.0 reduce-scatter.5.cloned.1.call-update
  263.9 0.0 all-reduce.5.cloned.1.call-start
  263.9 141.2 %reduce-scatter.3.cloned.1.call-done = f32[64,128]{1,0:T(8,128)} async-done(((f32[2048,128]{1,0:T(8,128)}), f32[64,128]{1,0:T(8,128)}) %reduce-scatter.3.cloned.1.call-update) | async-done | bytes 32784 | tf_op jit(solution)/shard_map/reduce_scatter | solution.py:73
  405.1 1.7 convolution_multiply_fusion
  406.8 52.2 %reduce-scatter.5.cloned.1.call-done = f32[128,3,128]{2,0,1:T(8,128)} async-done(((f32[1024,3,128]{2,0,1:T(8,128)}), f32[128,3,128]{2,0,1:T(8,128)}) %reduce-scatter.5.cloned.1.call-update) | async-done | bytes 196624 | tf_op jit(solution)/shard_map/reduce_scatter | solution.py:81
  458.9 2.0 convolution_bitcast_fusion.1
  460.9 0.0 all-reduce.5.cloned.1.call-update
  460.9 0.0 all-reduce.7.cloned.1.call-start
  461.0 305.7 %all-reduce.5.cloned.1.call-done = (f32[256,128]{1,0:T(8,128)}, f32[256,128]{1,0:T(8,128)}) async-done(((f32[256,128]{1,0:T(8,128)}, f32[256,128]{1,0:T(8,128)}), (f32[256,128]{1,0:T(8,128)}, f32[256,128]{1,0:T(8,128)})) %all-reduce.5.cloned.1.call-update) | async-done | bytes 262160 | tf_op jit(solution)/shard_map/psum | solution.py:90
  766.7 0.0 all-reduce.7.cloned.1.call-update
  766.7 83.4 %all-reduce.7.cloned.1.call-done = (f32[256,128]{1,0:T(8,128)}, f32[256,128]{1,0:T(8,128)}) async-done(((f32[256,128]{1,0:T(8,128)}, f32[256,128]{1,0:T(8,128)}), (f32[256,128]{1,0:T(8,128)}, f32[256,128]{1,0:T(8,128)})) %all-reduce.7.cloned.1.call-update) | async-done | bytes 262160 | tf_op jit(solution)/shard_map/psum | solution.py:90
  850.2 1.6 copy.22
  851.7 1.6 copy.23
  (7 shorter events, 0.0 us)
Async XLA Ops:
  7.2 1.6 copy-start
  7.2 155.0 %all-gather.5.cloned.1.call-start = ((), (), s32[]{:S(2)}) async-start(), calls=%async_computation.3 | async-start | bytes 1081344 | tf_op jit(solution)/shard_map/all_gather | solution.py:54
  12.9 192.4 %all-gather.3.cloned.1.call-start = ((), (), s32[]{:S(2)}) async-start(), calls=%async_computation.2 | async-start | bytes 1769472 | tf_op jit(solution)/shard_map/all_gather | solution.py:57
  18.1 387.0 %reduce-scatter.3.cloned.1.call-start = ((), (), s32[]{:S(2)}) async-start(), calls=%async_computation.4 | async-start | bytes 1081344 | tf_op jit(solution)/shard_map/reduce_scatter | solution.py:73
  237.8 13.5 %copy-start.2 = (bf16[1,2048,1024]{1,2,0:T(8,128)(2,1)S(1)}, bf16[1,2048,1024]{1,2,0:T(8,128)(2,1)}, u32[]{:S(2)}) copy-start(bf16[1,2048,1024]{1,2,0:T(8,128)(2,1)} %get-tuple-element.7) | copy-start | bytes 12582916
  237.8 13.5 %copy-start.5 = (bf16[2,3,1024,128]{3,2,1,0:T(8,128)(2,1)S(1)}, bf16[2,3,1024,128]{3,2,1,0:T(8,128)(2,1)}, u32[]{:S(2)}) copy-start(bf16[2,3,1024,128]{3,2,1,0:T(8,128)(2,1)} %all-gather.3.cloned.1.call-done) | copy-start | bytes 4718596
  248.1 2.0 copy-start.3
  248.1 3.2 copy-start.4
  251.4 5.0 copy-start.6
  256.3 202.7 %reduce-scatter.5.cloned.1.call-start = ((), (), s32[]{:S(2)}) async-start(), calls=%async_computation.5 | async-start | bytes 1769472 | tf_op jit(solution)/shard_map/reduce_scatter | solution.py:81
  256.3 597.0 %copy-start.1 = (bf16[4096,256]{1,0:T(8,128)(2,1)S(1)}, bf16[4096,256]{1,0:T(8,128)(2,1)}, u32[]{:S(2)}) copy-start(bf16[4096,256]{1,0:T(8,128)(2,1)} %param.11) | copy-start | bytes 6291460
  263.9 502.8 %all-reduce.5.cloned.1.call-start = ((), (), s32[]{:S(2)}) async-start(), calls=%async_computation.6 | async-start | bytes 524288 | tf_op jit(solution)/shard_map/psum | solution.py:90
  460.9 389.2 %all-reduce.7.cloned.1.call-start = ((), (), s32[]{:S(2)}) async-start(), calls=%async_computation.7 | async-start | bytes 524288 | tf_op jit(solution)/shard_map/psum | solution.py:90
Sparse Core Ops, SparseCore 0:
  13.0 149.1 all-gather.4
  164.0 41.2 all-gather.2
  256.4 148.6 reduce-scatter.2
  407.5 51.3 reduce-scatter.4
  462.0 304.6 all-reduce.4
  769.2 80.9 all-reduce.6
